TPU v7x, 128 devices: a whole 4x4x4 slice. The times are simulated.
128 devices in a mesh: rcv: 16 (over x_hi, y, core), src: 8 (over z, x_lo).
Axes of the slice: x: 4 (x_hi: 2, x_lo: 2; x = x_hi * 2 + x_lo), y: 4, z: 4, core: 2. Of those that a mesh axis runs over, the one named last changes fastest.
Arguments:
- kernel_codes: bfloat16 [2, 8192, 65536], P(None, 'rcv', 'src'), may hold values from -128 to 127
- kernel_exps: int32 [8192, 512], P('rcv', 'src'), may hold values from -17 to -14
- wavefield: bfloat16 [2, 65536, 128], P(None, 'src', 'rcv'), may hold values from -6 to 6
- observed: bfloat16 [2, 8192, 128], P(None, 'rcv'), may hold values from -6 to 6
- receiver_mask: int32 [8192], P('rcv'), may hold values 0 or 1
Outputs:
- residual: bfloat16 [2, 8192, 128], P(None, 'rcv', 'src')
- gradient: bfloat16 [2, 65536, 128], P(None, 'src', 'rcv')
All inputs are finite; a program needn't handle non-finite values. No bound on the sum of `receiver_mask` on one device may be relied on, other than what follows from the above.
Results may differ from a plain program's by a relative error of at most 0.0049.
Values may be sent and summed in bfloat16 or wider, within the bound.
No kernel may reach another device: no remote copies, remote signals or barrier semaphores. Data moves between devices by JAX's collectives and lax.ppermute only.
A program may use at most 128 MiB of HBM per device.

v0:
```python
import jax
import jax.numpy as jnp
from jax import lax
from jax.sharding import PartitionSpec as P

EXP_BLOCK = 128


def decode(codes, exps):
    rows = codes.shape[1]
    cols = codes.shape[2]
    scale = jnp.exp2(exps.astype(jnp.float32))[:, :, None]

    def widen(values):
        blocks = values.reshape(rows, cols // EXP_BLOCK, EXP_BLOCK).astype(jnp.float32) * scale
        return blocks.reshape(rows, cols).astype(jnp.bfloat16)

    return jnp.concatenate([widen(codes[0]), widen(codes[1])], axis=0)


def body(kernel_codes, kernel_exps, wavefield, observed, receiver_mask):
    rows = kernel_codes.shape[1]
    n_src = lax.axis_size("src")
    stacked = decode(kernel_codes, kernel_exps)
    piece = lax.all_gather(wavefield, "rcv", axis=2, tiled=True)
    span = piece.shape[2]
    joined = jnp.concatenate([piece[0], piece[1]], axis=1)
    prod = jnp.dot(stacked, joined, preferred_element_type=jnp.float32)
    pred_real = prod[:rows, :span] - prod[rows:, span:]
    pred_imag = prod[:rows, span:] + prod[rows:, :span]
    partial_pred = jnp.stack([pred_real, pred_imag])
    width = partial_pred.shape[2]
    share_cols = width // n_src
    live = receiver_mask.astype(jnp.float32)[None, :, None]
    predicted = lax.psum(partial_pred, "src")
    resid = (live * (predicted - observed.astype(jnp.float32))).astype(jnp.bfloat16)
    own_resid = lax.dynamic_slice_in_dim(resid, lax.axis_index("src") * share_cols, share_cols, 2)
    left = jnp.concatenate([resid[0], resid[1]], axis=0)
    right = jnp.concatenate([resid[1], -resid[0]], axis=0)
    grad_real = lax.dot_general(
        stacked, left, (((0,), (0,)), ((), ())), preferred_element_type=jnp.float32
    )
    grad_imag = lax.dot_general(
        stacked, right, (((0,), (0,)), ((), ())), preferred_element_type=jnp.float32
    )
    summed = lax.psum_scatter(
        jnp.stack([grad_real, grad_imag]), "rcv", scatter_dimension=2, tiled=True
    )
    gradient = summed.astype(jnp.bfloat16)
    return (own_resid, gradient)


def solution(mesh):
    in_specs = (
        P(None, "rcv", "src"),
        P("rcv", "src"),
        P(None, "src", "rcv"),
        P(None, "rcv", None),
        P("rcv"),
    )
    out_specs = (P(None, "rcv", "src"), P(None, "src", "rcv"))
    return jax.shard_map(body, mesh=mesh, in_specs=in_specs, out_specs=out_specs, check_vma=False)
```

profile of v0, /device:TPU:0, one launch (start us, length us, event | category | flops | bytes accessed | tf_op | source)
XLA Modules:
  0.0 313.3 jit_solution(1897431621627236321)
XLA Ops:
  7.2 0.0 all-gather.2.cloned.1.call-start
  7.2 0.7 all-gather.2.cloned.1.call-update
  7.9 0.0 all-reduce.4.cloned.1.call-start
  7.9 0.9 multiply_exponential_fusion
  8.9 0.1 copy.10
  9.0 4.6 %mul.30 = f32[512,64,128]{2,1,0:T(8,128)S(1)} broadcast(f32[512,64]{1,0:T(8,128)S(1)} %copy.10), dimensions={0,1} | broadcast | bytes 16908288 | tf_op jit(solution)/shard_map/mul | solution.py:15
  13.6 18.3 %fusion = (bf16[512,8192]{1,0:T(8,128)(2,1)}, bf16[512,8192]{1,0:T(8,128)(2,1)}) fusion(f32[64,8,64,128]{3,2,1,0:T(8,128)S(1)} %bitcast.33, bf16[2,512,8192]{2,1,0:T(8,128)(2,1)} %param.5), kind=kLoop, calls=%fused_computation.2 | loop fusion | flops 25165824 | bytes 50331648 | tf_op jit(solution)/shard_map/convert_element_type | solution.py:16
  32.0 35.8 %all-gather.2.cloned.1.call-done = bf16[2,8192,128]{1,2,0:T(8,128)(2,1)} async-done(((bf16[2,8192,8]{1,2,0:T(8,128)(2,1)}), bf16[2,8192,128]{1,2,0:T(8,128)(2,1)}) %all-gather.2.cloned.1.call-update) | async-done | bytes 4194320 | tf_op jit(solution)/shard_map/all_gather | solution.py:25
  67.7 4.1 %slice_bitcast_fusion.1 = (bf16[8192,128]{0,1:T(8,128)(2,1)S(1)}, bf16[8192,128]{0,1:T(8,128)(2,1)}) fusion(bf16[2,8192,128]{1,2,0:T(8,128)(2,1)} %all-gather.2.cloned.1.call-done), kind=kLoop, calls=%fused_computation.13 | loop fusion | bytes 8388608 | tf_op jit(solution)/shard_map/squeeze | solution.py:27
  71.8 1.3 copy-done
  73.1 9.5 %fusion.2 = f32[1024,256]{1,0:T(8,128)} fusion(bf16[512,8192]{1,0:T(8,128)(2,1)} %get-tuple-element.7, bf16[512,8192]{1,0:T(8,128)(2,1)S(1)} %copy-done, bf16[8192,128]{0,1:T(8,128)(2,1)} %get-tuple-element.9, bf16[8192,128]{0,1:T(8,128)(2,1)S(1)} %get-tuple-element.8), kind=kOutput, calls=%fused_computation.8 | convolution fusion | flops 4336910336 | bytes 22020096 | tf_op jit(solution)/shard_map/dot_general | solution.py:28
  82.7 1.2 fusion.7
  83.9 0.8 pad_maximum_fusion.5
  84.7 0.0 all-reduce.4.cloned.1.call-update
  84.8 0.0 copy-done.2
  84.8 0.0 copy-done.3
  84.8 0.6 dynamic-slice
  86.1 73.1 %all-reduce.4.cloned.1.call-done = f32[2,512,128]{2,1,0:T(8,128)} async-done(((f32[2,512,128]{2,1,0:T(8,128)}), f32[2,512,128]{2,1,0:T(8,128)}) %all-reduce.4.cloned.1.call-update) | async-done | bytes 524304 | tf_op jit(solution)/shard_map/psum | solution.py:35
  159.2 1.3 multiply_convert_fusion
  160.6 0.0 slice-start.1
  160.6 0.0 slice-start.3
  160.6 10.2 %convolution_bitcast_fusion.1 = f32[1,8192,128]{2,1,0:T(8,128)} fusion(bf16[512,8192]{1,0:T(8,128)(2,1)} %get-tuple-element.7, bf16[512,8192]{1,0:T(8,128)(2,1)} %get-tuple-element.6, bf16[512,128]{1,0:T(8,128)(2,1)S(1)} %get-tuple-element.13, bf16[512,128]{1,0:T(8,128)(2,1)S(1)} %get-tuple-element.12), kind=kOutput, calls=%fused_computation.6 | convolution fusion | flops 2181562368 | bytes 21233664 | tf_op jit(solution)/shard_map/dot_general | solution.py:40
  170.9 0.0 slice-done.1
  170.9 0.9 slice-done.3
  171.7 6.3 %convolution_bitcast_fusion = f32[1,8192,128]{2,1,0:T(8,128)} fusion(bf16[512,8192]{1,0:T(8,128)(2,1)S(1)} %bitcast.37, bf16[512,8192]{1,0:T(8,128)(2,1)S(1)} %bitcast.35, bf16[512,128]{1,0:T(8,128)(2,1)S(1)} %fusion.17, bf16[512,128]{1,0:T(8,128)(2,1)S(1)} %get-tuple-element.13), kind=kOutput, calls=%fused_computation.5 | convolution fusion | flops 2181562368 | bytes 21233664 | tf_op jit(solution)/shard_map/dot_general | solution.py:43
  178.0 7.2 %pad_maximum_fusion.1 = f32[2,8192,128]{2,1,0:T(8,128)} fusion(f32[1,8192,128]{2,1,0:T(8,128)} %convolution_bitcast_fusion, f32[1,8192,128]{2,1,0:T(8,128)} %convolution_bitcast_fusion.1), kind=kLoop, calls=%fused_computation.7 | loop fusion | flops 2097152 | bytes 16777216 | tf_op jit(solution)/shard_map/stack | solution.py:47
  185.2 13.2 %copy.11 = f32[2,8192,128]{1,0,2:T(2,128)} copy(f32[2,8192,128]{2,1,0:T(8,128)} %pad_maximum_fusion.1) | data formatting | bytes 16777216 | tf_op jit(solution)/shard_map/stack | solution.py:47
  198.4 105.1 %all-reduce.5 = bf16[2,8192,128]{1,0,2:T(2,128)(2,1)} all-reduce(f32[2,8192,128]{1,0,2:T(2,128)} %copy.11), channel_id=2, replica_groups=mesh['rcv'=16,'src'=8] {'rcv'}, use_global_device_ids=true, to_apply=%region_1.0.clone | all-reduce | flops 2097152 | bytes 12582912
  303.6 1.1 dynamic-slice_convert_fusion
  304.7 0.9 copy.13
  305.6 0.1 constant_dynamic-slice_fusion
  305.7 0.7 copy.12
  (14 shorter events, 0.1 us)
Async XLA Ops:
  7.2 60.6 %all-gather.2.cloned.1.call-start = ((), (), s32[]{:S(2)}) async-start(), calls=%async_computation | async-start | bytes 4456448 | tf_op jit(solution)/shard_map/all_gather | solution.py:25
  7.9 151.3 %all-reduce.4.cloned.1.call-start = ((), (), s32[]{:S(2)}) async-start(), calls=%async_computation.1 | async-start | bytes 1048576 | tf_op jit(solution)/shard_map/psum | solution.py:35
  67.7 5.4 %copy-start = (bf16[512,8192]{1,0:T(8,128)(2,1)S(1)}, bf16[512,8192]{1,0:T(8,128)(2,1)}, u32[]{:S(2)}) copy-start(bf16[512,8192]{1,0:T(8,128)(2,1)} %get-tuple-element.6) | copy-start | bytes 25165828
  73.1 11.7 %copy-start.2 = (s32[512]{0:T(512)S(1)}, s32[512]{0:T(512)}, u32[]{:S(2)}) copy-start(s32[512]{0:T(512)} %param.9) | copy-start | bytes 6148
  73.1 11.7 %copy-start.3 = (u32[128]{0:T(128)S(1)}, u32[128]{0:T(128)}, u32[]{:S(2)}) copy-start(u32[128]{0:T(128)} %constant.15) | copy-start | bytes 1540
  73.1 86.1 %copy-start.1 = (bf16[2,512,128]{2,1,0:T(8,128)(2,1)S(1)}, bf16[2,512,128]{2,1,0:T(8,128)(2,1)}, u32[]{:S(2)}) copy-start(bf16[2,512,128]{2,1,0:T(8,128)(2,1)} %param.8) | copy-start | bytes 786436
  159.2 11.6 %slice-start = ((s8[8388608]{0:T(1024)(128)(4,1)}), s8[4194304]{0:T(1024)(128)(4,1)S(1)}, s32[]{:S(2)}) async-start(s8[8388608]{0:T(1024)(128)(4,1)} %bitcast.34), calls=%async_computation.2 | async-start | bytes 8388608
  159.2 11.6 %slice-start.2 = ((s8[8388608]{0:T(1024)(128)(4,1)}), s8[4194304]{0:T(1024)(128)(4,1)S(1)}, s32[]{:S(2)}) async-start(s8[8388608]{0:T(1024)(128)(4,1)} %bitcast.36), calls=%async_computation.4 | async-start | bytes 8388608
  160.6 10.3 %slice-start.1 = ((s8[8388608]{0:T(1024)(128)(4,1)}), s8[4194304]{0:T(1024)(128)(4,1)S(1)}, s32[]{:S(2)}) async-start(s8[8388608]{0:T(1024)(128)(4,1)} %bitcast.34), calls=%async_computation.3 | async-start | bytes 8388608
  160.6 11.1 %slice-start.3 = ((s8[8388608]{0:T(1024)(128)(4,1)}), s8[4194304]{0:T(1024)(128)(4,1)S(1)}, s32[]{:S(2)}) async-start(s8[8388608]{0:T(1024)(128)(4,1)} %bitcast.36), calls=%async_computation.5 | async-start | bytes 8388608
Sparse Core Ops, SparseCore 0:
  10.5 57.1 all-gather.1
  84.9 74.2 all-reduce.3
where the time goes:
time: 314 us; the launch traced here: 313 us
  waiting for transfers between devices  110 us (35%)
  blocking collectives  105 us (33%)
  other arithmetic  29.9 us (10%)
  local copies, waits for them, and re-layouts  27.7 us (9%)
  matrix products  26 us (8%)
  between operations  14.8 us (5%)
    unnamed x1, blocking collectives  105 us
    psum x1, waiting for transfers between devices, body(): predicted = lax.psum(partial_pred, 'src')  73.1 us
    all_gather x1, waiting for transfers between devices, body(): piece = lax.all_gather(wavefield, 'rcv', axis=2, tiled=True)  35.8 us
    convert_element_type x1, other arithmetic, widen(): return blocks.reshape(rows, cols).astype(jnp.bfloat16)  18.3 us
    another operation x1, local copies, waits for them, and re-layouts, body(): jnp.stack([grad_real, grad_imag])  13.2 us
    dot_general x1, matrix products, body(): lax.dot_general(stacked, left, (((0,), (0,)), ((), ())), preferred_elemen...  10.2 us
    dot_general x1, matrix products, body(): prod = jnp.dot(stacked, joined, preferred_element_type=jnp.float32)  9.54 us
    another operation x1, other arithmetic, body(): jnp.stack([grad_real, grad_imag])  7.24 us
  transfers between devices with their start and end apart: 2, of which 2 were waited for; matrix products, arithmetic and copies ran while one was open for 8% of the time, Pallas kernels for 0%

commit v1 on v0

--- a/solution.py
+++ b/solution.py
@@ -22,7 +22,9 @@
     rows = kernel_codes.shape[1]
     n_src = lax.axis_size("src")
     stacked = decode(kernel_codes, kernel_exps)
-    piece = lax.all_gather(wavefield, "rcv", axis=2, tiled=True)
+    piece = jnp.concatenate(
+        lax.all_to_all(jnp.stack([wavefield] * lax.axis_size("rcv")), "rcv", 0, 0), axis=2
+    )
     span = piece.shape[2]
     joined = jnp.concatenate([piece[0], piece[1]], axis=1)
     prod = jnp.dot(stacked, joined, preferred_element_type=jnp.float32)

time: 314 us -> 330 us (1.051)
  starting transfers between devices: 0.08 us -> 7.24 us
  waiting for transfers between devices: 110 us -> 116 us
    all_gather x1 -> x0, waiting for transfers between devices: 35.8 us -> none  [body(): piece = lax.all_gather(wavefield, 'rcv', axis=2, tiled=True)]
    all_to_all x0 -> x1, waiting for transfers between devices: none -> 32.7 us  [body(): lax.all_to_all(jnp.stack([wavefield] * lax.axis_size('rcv')), 'rcv', 0, 0)]
    psum x1, waiting for transfers between devices: 73.1 us -> 83.1 us  [body(): predicted = lax.psum(partial_pred, 'src')]
    all_to_all x0 -> x1, starting transfers between devices: none -> 7.2 us  [body(): lax.all_to_all(jnp.stack([wavefield] * lax.axis_size('rcv')), 'rcv', 0, 0)]
    another operation x0 -> x1, local copies, waits for them, and re-layouts: none -> 3.44 us  [body(): jnp.stack([wavefield] * lax.axis_size('rcv'))]
  transfers between devices with their start and end apart: 2 -> 2, of which waited for: 2 -> 2; matrix products, arithmetic and copies ran while one was open for 8% -> 7% of each run, Pallas kernels for 0% -> 0%
where the time goes in v1:
time: 330 us; the launch traced here: 329 us
  waiting for transfers between devices  116 us (35%)
  blocking collectives  105 us (32%)
  local copies, waits for them, and re-layouts  30.7 us (9%)
  other arithmetic  29 us (9%)
  matrix products  26.3 us (8%)
  between operations  14.9 us (5%)
  starting transfers between devices  7.24 us (2%)
    unnamed x1, blocking collectives  105 us
    psum x1, waiting for transfers between devices, body(): predicted = lax.psum(partial_pred, 'src')  83.1 us
    all_to_all x1, waiting for transfers between devices, body(): lax.all_to_all(jnp.stack([wavefield] * lax.axis_size('rcv')), 'rcv', 0, 0)  32.7 us
    convert_element_type x1, other arithmetic, widen(): return blocks.reshape(rows, cols).astype(jnp.bfloat16)  18.3 us
    another operation x1, local copies, waits for them, and re-layouts, body(): jnp.stack([grad_real, grad_imag])  13.3 us
    dot_general x1, matrix products, body(): lax.dot_general(stacked, left, (((0,), (0,)), ((), ())), preferred_elemen...  10.5 us
    dot_general x1, matrix products, body(): prod = jnp.dot(stacked, joined, preferred_element_type=jnp.float32)  9.54 us
    another operation x1, other arithmetic, body(): jnp.stack([grad_real, grad_imag])  7.24 us
  transfers between devices with their start and end apart: 2, of which 2 were waited for; matrix products, arithmetic and copies ran while one was open for 7% of the time, Pallas kernels for 0%

profile of v1, /device:TPU:0, one launch (start us, length us, event | category | flops | bytes accessed | tf_op | source)
XLA Modules:
  0.0 329.0 jit_solution(3009141171338126210)
XLA Ops:
  7.2 3.4 %stack.14 = bf16[16,2,8192,8]{2,3,1,0:T(8,128)(2,1)} broadcast(bf16[2,8192,8]{1,2,0:T(8,128)(2,1)} %param.7), dimensions={1,2,3} | broadcast | bytes 4456448 | tf_op jit(solution)/shard_map/stack | solution.py:26
  10.6 7.2 %all-to-all-start = ((bf16[16,2,8192,8]{2,3,1,0:T(8,128)(2,1)}), bf16[16,2,8192,8]{2,3,1,0:T(8,128)(2,1)}, u32[]{:S(2)}, u32[]{:S(2)}) async-start(bf16[16,2,8192,8]{2,3,1,0:T(8,128)(2,1)} %stack.14), calls=%async_computation | async-start | bytes 8388608 | tf_op jit(solution)/shard_map/all_to_all | solution.py:26
  17.8 0.0 all-reduce.4.cloned.1.call-start
  17.9 0.1 copy.14
  18.0 4.6 %mul.30 = f32[512,64,128]{2,1,0:T(8,128)S(1)} broadcast(f32[512,64]{1,0:T(8,128)S(1)} %copy.14), dimensions={0,1} | broadcast | bytes 16908288 | tf_op jit(solution)/shard_map/mul | solution.py:15
  22.7 18.3 %fusion = (bf16[512,8192]{1,0:T(8,128)(2,1)}, bf16[512,8192]{1,0:T(8,128)(2,1)}) fusion(f32[64,8,64,128]{3,2,1,0:T(8,128)S(1)} %bitcast.36, bf16[2,512,8192]{2,1,0:T(8,128)(2,1)} %param.5), kind=kLoop, calls=%fused_computation.2 | loop fusion | flops 25165824 | bytes 50331648 | tf_op jit(solution)/shard_map/convert_element_type | solution.py:16
  41.0 32.7 %all-to-all-done = bf16[16,2,8192,8]{2,3,1,0:T(8,128)(2,1)} async-done(((bf16[16,2,8192,8]{2,3,1,0:T(8,128)(2,1)}), bf16[16,2,8192,8]{2,3,1,0:T(8,128)(2,1)}, u32[]{:S(2)}, u32[]{:S(2)}) %all-to-all-start) | async-done | bytes 4194336 | tf_op jit(solution)/shard_map/all_to_all | solution.py:26
  73.7 2.6 copy.23
  76.3 0.0 slice-start.1
  76.3 1.6 slice_bitcast_fusion.1
  78.0 1.5 slice-done.1
  79.5 9.5 %fusion.2 = f32[1024,256]{1,0:T(8,128)} fusion(bf16[512,8192]{1,0:T(8,128)(2,1)} %get-tuple-element.9, bf16[512,8192]{1,0:T(8,128)(2,1)S(1)} %bitcast.39, bf16[8192,128]{0,1:T(8,128)(2,1)} %get-tuple-element.11, bf16[8192,128]{0,1:T(8,128)(2,1)S(1)} %get-tuple-element.10), kind=kOutput, calls=%fused_computation.8 | convolution fusion | flops 4336910336 | bytes 22020096 | tf_op jit(solution)/shard_map/dot_general | solution.py:30
  89.0 1.2 fusion.7
  90.2 0.8 pad_maximum_fusion.5
  91.1 0.0 all-reduce.4.cloned.1.call-update
  91.1 0.0 copy-done.2
  91.1 0.0 copy-done.3
  91.2 0.6 dynamic-slice
  92.4 83.1 %all-reduce.4.cloned.1.call-done = f32[2,512,128]{2,1,0:T(8,128)} async-done(((f32[2,512,128]{2,1,0:T(8,128)}), f32[2,512,128]{2,1,0:T(8,128)}) %all-reduce.4.cloned.1.call-update) | async-done | bytes 524304 | tf_op jit(solution)/shard_map/psum | solution.py:37
  175.5 0.0 copy-done
  175.5 1.3 multiply_convert_fusion
  176.9 0.0 slice-start.3
  176.9 0.0 slice-start.5
  176.9 10.5 %convolution_bitcast_fusion.1 = f32[1,8192,128]{2,1,0:T(8,128)} fusion(bf16[512,8192]{1,0:T(8,128)(2,1)} %get-tuple-element.9, bf16[512,8192]{1,0:T(8,128)(2,1)} %get-tuple-element.8, bf16[512,128]{1,0:T(8,128)(2,1)S(1)} %get-tuple-element.15, bf16[512,128]{1,0:T(8,128)(2,1)S(1)} %get-tuple-element.14), kind=kOutput, calls=%fused_computation.6 | convolution fusion | flops 2181562368 | bytes 21233664 | tf_op jit(solution)/shard_map/dot_general | solution.py:42
  187.4 6.3 %convolution_bitcast_fusion = f32[1,8192,128]{2,1,0:T(8,128)} fusion(bf16[512,8192]{1,0:T(8,128)(2,1)S(1)} %bitcast.43, bf16[512,8192]{1,0:T(8,128)(2,1)S(1)} %bitcast.41, bf16[512,128]{1,0:T(8,128)(2,1)S(1)} %fusion.17, bf16[512,128]{1,0:T(8,128)(2,1)S(1)} %get-tuple-element.15), kind=kOutput, calls=%fused_computation.5 | convolution fusion | flops 2181562368 | bytes 21233664 | tf_op jit(solution)/shard_map/dot_general | solution.py:45
  193.7 7.2 %pad_maximum_fusion.1 = f32[2,8192,128]{2,1,0:T(8,128)} fusion(f32[1,8192,128]{2,1,0:T(8,128)} %convolution_bitcast_fusion, f32[1,8192,128]{2,1,0:T(8,128)} %convolution_bitcast_fusion.1), kind=kLoop, calls=%fused_computation.7 | loop fusion | flops 2097152 | bytes 16777216 | tf_op jit(solution)/shard_map/stack | solution.py:49
  200.9 13.3 %copy.16 = f32[2,8192,128]{1,0,2:T(2,128)} copy(f32[2,8192,128]{2,1,0:T(8,128)} %pad_maximum_fusion.1) | data formatting | bytes 16777216 | tf_op jit(solution)/shard_map/stack | solution.py:49
  214.2 105.1 %all-reduce.5 = bf16[2,8192,128]{1,0,2:T(2,128)(2,1)} all-reduce(f32[2,8192,128]{1,0,2:T(2,128)} %copy.16), channel_id=2, replica_groups=mesh['rcv'=16,'src'=8] {'rcv'}, use_global_device_ids=true, to_apply=%region_1.0.clone | all-reduce | flops 2097152 | bytes 12582912
  319.3 1.1 dynamic-slice_convert_fusion
  320.4 0.9 copy.18
  321.3 0.1 constant_dynamic-slice_fusion
  321.4 0.7 copy.17
  (20 shorter events, 0.1 us)
Async XLA Ops:
  7.2 10.7 %copy-start.1 = (s32[512,64]{0,1:T(8,128)S(1)}, s32[512,64]{0,1:T(8,128)}, u32[]{:S(2)}) copy-start(s32[512,64]{0,1:T(8,128)} %param.6) | copy-start | bytes 393220
  10.6 63.1 %all-to-all-start = ((bf16[16,2,8192,8]{2,3,1,0:T(8,128)(2,1)}), bf16[16,2,8192,8]{2,3,1,0:T(8,128)(2,1)}, u32[]{:S(2)}, u32[]{:S(2)}) async-start(bf16[16,2,8192,8]{2,3,1,0:T(8,128)(2,1)} %stack.14), calls=%async_computation | async-start | bytes 8388608 | tf_op jit(solution)/shard_map/all_to_all | solution.py:26
  17.8 157.6 %all-reduce.4.cloned.1.call-start = ((), (), s32[]{:S(2)}) async-start(), calls=%async_computation.1 | async-start | bytes 1048576 | tf_op jit(solution)/shard_map/psum | solution.py:37
  73.7 4.3 %slice-start = ((s8[8388608]{0:T(1024)(128)(4,1)}), s8[4194304]{0:T(1024)(128)(4,1)S(1)}, s32[]{:S(2)}) async-start(s8[8388608]{0:T(1024)(128)(4,1)} %bitcast.38), calls=%async_computation.2 | async-start | bytes 8388608
  76.3 3.2 slice-start.1
  79.5 11.7 %copy-start.2 = (s32[512]{0:T(512)S(1)}, s32[512]{0:T(512)}, u32[]{:S(2)}) copy-start(s32[512]{0:T(512)} %param.9) | copy-start | bytes 6148
  79.5 11.7 %copy-start.3 = (u32[128]{0:T(128)S(1)}, u32[128]{0:T(128)}, u32[]{:S(2)}) copy-start(u32[128]{0:T(128)} %constant.15) | copy-start | bytes 1540
  79.5 96.0 %copy-start = (bf16[2,512,128]{2,1,0:T(8,128)(2,1)S(1)}, bf16[2,512,128]{2,1,0:T(8,128)(2,1)}, u32[]{:S(2)}) copy-start(bf16[2,512,128]{2,1,0:T(8,128)(2,1)} %param.8) | copy-start | bytes 786436
  175.5 11.9 %slice-start.2 = ((s8[8388608]{0:T(1024)(128)(4,1)}), s8[4194304]{0:T(1024)(128)(4,1)S(1)}, s32[]{:S(2)}) async-start(s8[8388608]{0:T(1024)(128)(4,1)} %bitcast.40), calls=%async_computation.4 | async-start | bytes 8388608
  175.5 11.9 %slice-start.4 = ((s8[8388608]{0:T(1024)(128)(4,1)}), s8[4194304]{0:T(1024)(128)(4,1)S(1)}, s32[]{:S(2)}) async-start(s8[8388608]{0:T(1024)(128)(4,1)} %bitcast.42), calls=%async_computation.6 | async-start | bytes 8388608
  176.9 10.5 %slice-start.3 = ((s8[8388608]{0:T(1024)(128)(4,1)}), s8[4194304]{0:T(1024)(128)(4,1)S(1)}, s32[]{:S(2)}) async-start(s8[8388608]{0:T(1024)(128)(4,1)} %bitcast.40), calls=%async_computation.5 | async-start | bytes 8388608
  176.9 10.5 %slice-start.5 = ((s8[8388608]{0:T(1024)(128)(4,1)}), s8[4194304]{0:T(1024)(128)(4,1)S(1)}, s32[]{:S(2)}) async-start(s8[8388608]{0:T(1024)(128)(4,1)} %bitcast.42), calls=%async_computation.7 | async-start | bytes 8388608
Sparse Core Ops, SparseCore 0:
  91.2 84.1 all-reduce.3
